TPU v7x, 256 devices: a whole 4x4x8 slice. The times are simulated.
256 devices in a mesh: ctx: 32 (over z, y_hi, core), head: 8 (over y_lo, x).
Axes of the slice: x: 4, y: 4 (y_hi: 2, y_lo: 2; y = y_hi * 2 + y_lo), z: 8, core: 2. Of those that a mesh axis runs over, the one named last changes fastest.
Arguments:
- query1: bfloat16 [16384, 6144], P('ctx', 'head'), may hold values from -6 to 6
- key1: bfloat16 [16384, 6144], P('ctx', 'head'), may hold values from -6 to 6
- value1: bfloat16 [16384, 6144], P('ctx', 'head'), may hold values from -50 to 50
- log_decay: float32 [16384, 64], P('ctx', 'head'), may hold values from -1 to 0
- out_weight: bfloat16 [6144, 3072], P('head'), may hold values from -0.078125 to 0.078125
- query2: bfloat16 [16384, 6144], P('ctx', 'head'), may hold values from -12 to 12
- key2: bfloat16 [16384, 6144], P('ctx', 'head'), may hold values from -6 to 6
- value2: bfloat16 [16384, 6144], P('ctx', 'head'), may hold values from -6 to 6
Outputs:
- linear_mixed: bfloat16 [16384, 3072], P(('ctx', 'head'))
- attended: bfloat16 [16384, 6144], P('ctx', 'head')
All inputs are finite; a program needn't handle non-finite values.
Results may differ from a plain program's by a relative error of at most 0.017.
Values may be sent and summed in bfloat16 or wider, within the bound.
A program may use at most 64 MiB of HBM per device.

v0:
```python
import math
import jax
import jax.numpy as jnp
from jax import lax
from jax.sharding import PartitionSpec as P

DH = 96
LBLOCK = 256
eps_norm = 1e-06


def passed_along(value, axis, steps):
    count = lax.axis_size(axis)
    initial, last = (max(0, -steps), min(count, count - steps))
    return lax.ppermute(value, axis, [(source, source + steps) for source in range(initial, last)])


def block_step(carry_state, pieces):
    query_part, key_part, value_part, decay_part = pieces
    block_len = decay_part.shape[0]
    running = jnp.cumsum(decay_part, axis=0)
    by_head = running.T
    gaps_log = by_head[:, :, None] - by_head[:, None, :]
    causal = jnp.arange(block_len)[:, None] >= jnp.arange(block_len)[None, :]
    weight = jnp.exp(jnp.where(causal[None], gaps_log, -jnp.inf))
    scores = jnp.einsum("ihd,jhd->hij", query_part, key_part, preferred_element_type=jnp.float32)
    mixing = (scores * weight).astype(jnp.bfloat16)
    inside = jnp.einsum("hij,jhd->ihd", mixing, value_part, preferred_element_type=jnp.float32)
    outside = jnp.einsum(
        "ihd,hde->ihe",
        query_part.astype(jnp.float32) * jnp.exp(running)[:, :, None],
        carry_state,
        precision=lax.Precision.HIGHEST,
    )
    block_total = running[-1]
    update = jnp.einsum(
        "jhd,jhe->hde",
        key_part.astype(jnp.float32) * jnp.exp(block_total[None, :] - running)[:, :, None],
        value_part.astype(jnp.float32),
        precision=lax.Precision.HIGHEST,
    )
    new_state = jnp.exp(block_total)[:, None, None] * carry_state + update
    return (new_state, inside + outside)


def per_device(query1, key1, value1, log_decay, out_weight, query2, key2, value2):
    tok_rows = query1.shape[0]
    head_count = log_decay.shape[1]
    head_size = DH
    block_count = tok_rows // LBLOCK
    inputs = (
        query1.reshape(block_count, LBLOCK, head_count, head_size),
        key1.reshape(block_count, LBLOCK, head_count, head_size),
        value1.reshape(block_count, LBLOCK, head_count, head_size),
        log_decay.reshape(block_count, LBLOCK, head_count),
    )
    empty_state = jnp.zeros((head_count, head_size, head_size), jnp.float32)
    state_dev, outputs = lax.scan(block_step, empty_state, inputs)
    local_out = outputs.reshape(tok_rows, head_count, head_size)
    decay_dev = jnp.cumsum(log_decay, axis=0)
    device_total = decay_dev[-1]
    position = lax.axis_index("ctx")
    totals = lax.all_gather(device_total[None, :], "ctx", axis=0, tiled=True)
    device_ids = jnp.arange(totals.shape[0], dtype=jnp.int32)[:, None]
    earlier_rows = device_ids < position
    running = jnp.cumsum(totals, axis=0)
    before_sum = jnp.sum(jnp.where(earlier_rows, totals, 0.0), axis=0)
    weights = jnp.exp(jnp.where(earlier_rows, before_sum[None, :] - running, -jnp.inf))
    incoming = empty_state + jnp.einsum(
        "nh,nhde->hde",
        weights,
        lax.all_gather(state_dev[None].astype(jnp.bfloat16), "ctx", axis=0, tiled=True).astype(
            jnp.float32
        ),
        precision=lax.Precision.HIGHEST,
    )
    correction = jnp.einsum(
        "ihd,hde->ihe",
        query1.reshape(tok_rows, head_count, head_size).astype(jnp.float32)
        * jnp.exp(decay_dev)[:, :, None],
        incoming,
        precision=lax.Precision.HIGHEST,
    )
    combined = local_out + correction
    mean_square = jnp.mean(combined * combined, axis=-1, keepdims=True)
    normed = (
        (combined / jnp.sqrt(mean_square + eps_norm))
        .astype(jnp.bfloat16)
        .reshape(tok_rows, head_count * head_size)
    )
    linear_mixed = lax.psum_scatter(
        jnp.dot(normed, out_weight, preferred_element_type=jnp.float32).astype(jnp.bfloat16),
        "head",
        scatter_dimension=0,
        tiled=True,
    )
    stacked = jnp.stack((key2, value2))
    received = []
    moving = stacked
    for distance in range(3):
        moving = passed_along(moving, "ctx", 1)
        received.append(moving)
    window_keys = jnp.concatenate([received[2], received[1], received[0], stacked], axis=1)
    heads_soft = query2.shape[1] // head_size
    query_rows = min(512, tok_rows)
    key_span = 3 * tok_rows + query_rows
    score_scale = 1.0 / math.sqrt(DH)
    lowest_key = (3 - position) * tok_rows

    def attend_block(block_index):
        first_row = block_index * query_rows
        query_part = query2.reshape(query_rows, heads_soft, head_size)
        key_part = window_keys[0].reshape(key_span, heads_soft, head_size)
        value_part = window_keys[1].reshape(key_span, heads_soft, head_size)
        scores = (
            jnp.einsum("ihd,jhd->hij", query_part, key_part, preferred_element_type=jnp.float32)
            * score_scale
        )
        query_pos = first_row + jnp.arange(query_rows, dtype=jnp.int32)[:, None]
        key_pos = first_row + jnp.arange(key_span, dtype=jnp.int32)[None, :]
        allowed = (
            (key_pos > query_pos) & (key_pos <= 3 * tok_rows + query_pos) & (key_pos >= lowest_key)
        )
        scores = jnp.where(allowed[None], scores, -jnp.inf)
        row_peak = jnp.max(scores, axis=-1, keepdims=True)
        exponent = jnp.exp(scores - row_peak)
        probability = (exponent / jnp.sum(exponent, axis=-1, keepdims=True)).astype(jnp.bfloat16)
        result = jnp.einsum(
            "hij,jhd->ihd", probability, value_part, preferred_element_type=jnp.float32
        )
        return result.astype(jnp.bfloat16).reshape(query_rows, heads_soft * head_size)

    attended = lax.map(attend_block, jnp.arange(tok_rows // query_rows, dtype=jnp.int32))
    attended = attended.reshape(tok_rows, heads_soft * head_size)
    return (linear_mixed, attended)


def solution(mesh):
    in_specs = (
        P("ctx", "head"),
        P("ctx", "head"),
        P("ctx", "head"),
        P("ctx", "head"),
        P("head", None),
        P("ctx", "head"),
        P("ctx", "head"),
        P("ctx", "head"),
    )
    out_specs = (P(("ctx", "head"), None), P("ctx", "head"))
    return jax.shard_map(
        per_device, mesh=mesh, in_specs=in_specs, out_specs=out_specs, check_vma=False
    )
```

profile of v0, /device:TPU:1, one launch (start us, length us, event | category | flops | bytes accessed | tf_op | source)
XLA Modules:
  0.0 302.6 jit_solution(10613626920884037711)
XLA Ops:
  7.2 2.2 reshape.198
  10.2 2.2 reshape.199
  13.1 3.0 reshape.200
  16.1 1.6 copy.60
  17.8 51.9 %while.4 = (s32[]{:T(128)}, f32[8,96,96]{2,1,0:T(8,128)S(1)}, f32[2,256,8,96]{1,0,3,2:T(2,128)}, f32[2,256,8]{1,2,0:T(8,128)}, bf16[2,256,8,96]{1,3,2,0:T(8,128)...) while((s32[]{:T(128)}, f32[8,96,96]{2,1,0:T(8,128)S(1)}, ...), condition=%wide.region_3.4_spmd.clone, body=%wide.region_0.3_spmd.clone.sunk | while | flops 658018304 | bytes 9203808 | solution.py:58
  20.5 1.7 fusion.98
  23.6 1.7 fusion.99
  26.1 16.7 %dynamic_update_slice.9 = f32[2,256,8,96]{1,0,3,2:T(2,128)} dynamic-update-slice(f32[2,256,8,96]{1,0,3,2:T(2,128)} %get-tuple-element.191, f32[1,256,8,96]{1,0,3,2:T(1,128)S(1)} %copy.94, s32[]{:T(128)} %get-tuple-element.189, s32[]{:T(128)} %constant.60.clone.1..sunk, s32[]{:T(128)} %constant.60.clone.1..sunk, s32[]{:T(128)} %constant.60.clone.1..sunk) | dynamic-update-slice | bytes 1572868 | tf_op jit(solution)/shard_map/while/body/jit(dynamic_update_index_in_dim)/dynamic_update_slice | solution.py:58
  46.4 1.7 fusion.98
  49.5 1.7 fusion.99
  52.0 16.7 %dynamic_update_slice.9 = f32[2,256,8,96]{1,0,3,2:T(2,128)} dynamic-update-slice(f32[2,256,8,96]{1,0,3,2:T(2,128)} %get-tuple-element.191, f32[1,256,8,96]{1,0,3,2:T(1,128)S(1)} %copy.94, s32[]{:T(128)} %get-tuple-element.189, s32[]{:T(128)} %constant.60.clone.1..sunk, s32[]{:T(128)} %constant.60.clone.1..sunk, s32[]{:T(128)} %constant.60.clone.1..sunk) | dynamic-update-slice | bytes 1572868 | tf_op jit(solution)/shard_map/while/body/jit(dynamic_update_index_in_dim)/dynamic_update_slice | solution.py:58
  70.5 2.7 pad_maximum_fusion
  73.2 6.2 %collective-permute-start = (bf16[2,512,768]{2,1,0:T(8,128)(2,1)}, bf16[2,512,768]{2,1,0:T(8,128)(2,1)}, u32[]{:S(2)}, u32[]{:S(2)}) collective-permute-start(bf16[2,512,768]{2,1,0:T(8,128)(2,1)} %pad_maximum_fusion), channel_id=1, source_target_pairs={{0,8},{8,16},{16,24},{24,32},{32,40},{40,48},{48,56},{56,64},{64,7... | collective-permute-start | bytes 4718600 | tf_op jit(solution)/shard_map/ppermute | solution.py:15
  79.7 2.2 reduce-window.16
  82.3 52.6 %all-gather.1 = f32[32,1,8]{2,1,0:T(1,128)S(1)} all-gather(f32[1,1,8]{2,1,0:T(1,128)S(1)} %bitcast.146), channel_id=1, replica_groups=mesh['ctx'=32,'head'=8] {'ctx'}, dimensions={0}, use_global_device_ids=true | all-gather | bytes 1056 | tf_op jit(solution)/shard_map/all_gather | solution.py:63
  135.0 2.5 reshape.184
  137.8 2.1 collective-permute-start.1
  139.9 45.3 %all-gather.4.cloned.1.call-done = bf16[256,96,96]{2,1,0:T(8,128)(2,1)} async-done(((bf16[8,96,96]{2,1,0:T(8,128)(2,1)}), bf16[256,96,96]{2,1,0:T(8,128)(2,1)}) %all-gather.4.cloned.1.call-update) | async-done | bytes 4718608 | tf_op jit(solution)/shard_map/all_gather | solution.py:72
  185.1 4.5 %multiply_reduce_fusion = f32[8,96,96]{2,1,0:T(8,128)S(1)} fusion(bf16[8,32,96,96]{3,2,0,1:T(8,128)(2,1)} %bitcast.131, f32[8,32]{0,1:T(8,128)S(1)} %exponential_bitcast_fusion), kind=kLoop, calls=%fused_computation.53 | loop fusion | flops 7004160 | bytes 5014528 | tf_op jit(solution)/shard_map/nh,nhde->hde/dot_general | solution.py:69
  189.6 1.6 multiply_reduce_fusion.1
  191.5 6.4 %convolution_convert_fusion = bf16[512,3072]{1,0:T(8,128)(2,1)} fusion(bf16[512,768]{0,1:T(8,128)(2,1)S(1)} %bitcast.143, bf16[768,3072]{1,0:T(8,128)(2,1)} %param.14), kind=kOutput, calls=%fused_computation.57 | convolution fusion | flops 2417491968 | bytes 8650752 | tf_op jit(solution)/shard_map/dot_general | solution.py:92
  197.9 2.1 collective-permute-start.2
  200.0 2.3 copy.65
  202.3 2.0 fusion.46
  204.3 42.8 %collective-permute-done.2 = bf16[2,512,768]{2,1,0:T(8,128)(2,1)S(1)} collective-permute-done((bf16[2,512,768]{2,1,0:T(8,128)(2,1)}, bf16[2,512,768]{2,1,0:T(8,128)(2,1)S(1)}, u32[]{:S(2)}, u32[]{:S(2)}) %collective-permute-start.2) | collective-permute-done | bytes 1572896 | tf_op jit(solution)/shard_map/ppermute | solution.py:15
  247.1 2.8 maximum_maximum_fusion
  249.9 2.1 fusion.66
  252.0 4.7 %copy.64 = bf16[1,2048,768]{1,2,0:T(8,128)(2,1)} copy(bf16[1,2048,768]{2,1,0:T(8,128)(2,1)} %get-tuple-element.128) | data formatting | bytes 6291456 | tf_op jit(solution)/shard_map/while/body/eval_jaxpr/slice | solution.py:113
  256.7 3.0 copy.63
  259.7 14.4 %fusion.67 = f32[8,512]{1,0:T(8,128)S(1)} fusion(pred[512,2048]{0,1:T(8,128)(4,1)} %fusion.46, bf16[2048,8,96]{0,2,1:T(8,128)(2,1)} %bitcast.132, bf16[512,8,96]{0,2,1:T(8,128)(2,1)} %bitcast.140), kind=kOutput, calls=%fused_computation.85 | convolution fusion | flops 1644169216 | bytes 4997120 | tf_op jit(solution)/shard_map/while/body/eval_jaxpr/sub | solution.py:126
  274.2 19.3 %fusion.54 = bf16[8,96,512]{2,1,0:T(8,128)(2,1)} fusion(bf16[2048,8,96]{0,2,1:T(8,128)(2,1)S(1)} %bitcast.134, f32[8,512]{1,0:T(8,128)S(1)} %fusion.67, pred[512,2048]{0,1:T(8,128)(4,1)} %fusion.46, bf16[2048,8,96]{0,2,1:T(8,128)(2,1)} %bitcast.133, bf16[512,8,96]{0,2,1:T(8,128)(2,1)} %bitcast.141), kind=kOutput, calls=%fused_computation.67 | convolution fusion | flops 3263567872 | bytes 8929280 | tf_op jit(solution)/shard_map/while/body/eval_jaxpr/hij,jhd->ihd/dot_general | solution.py:128
  293.5 2.3 copy.67
  (64 shorter events, 15.1 us)
Async XLA Ops:
  7.2 178.0 %all-gather.4.cloned.1.call-start = ((), (), s32[]{:S(2)}) async-start(), calls=%async_computation.2 | async-start | bytes 6488064 | tf_op jit(solution)/shard_map/all_gather | solution.py:72
  19.3 0.6 copy-start.4
  45.2 0.6 copy-start.4
  69.7 9.7 %copy-start = (bf16[512,768]{1,0:T(8,128)(2,1)S(1)}, bf16[512,768]{1,0:T(8,128)(2,1)}, u32[]{:S(2)}) copy-start(bf16[512,768]{1,0:T(8,128)(2,1)} %param.10) | copy-start | bytes 2359300
  70.4 225.3 %reduce-scatter.2.cloned.1.call-start = ((), (), s32[]{:S(2)}) async-start(), calls=%async_computation.1 | async-start | bytes 3538944 | tf_op jit(solution)/shard_map/reduce_scatter | solution.py:91
  73.2 64.6 %collective-permute-start = (bf16[2,512,768]{2,1,0:T(8,128)(2,1)}, bf16[2,512,768]{2,1,0:T(8,128)(2,1)}, u32[]{:S(2)}, u32[]{:S(2)}) collective-permute-start(bf16[2,512,768]{2,1,0:T(8,128)(2,1)} %pad_maximum_fusion), channel_id=1, source_target_pairs={{0,8},{8,16},{16,24},{24,32},{32,40},{40,48},{48,56},{56,64},{64,7... | collective-permute-start | bytes 4718600 | tf_op jit(solution)/shard_map/ppermute | solution.py:15
  137.8 60.1 %collective-permute-start.1 = (bf16[2,512,768]{2,1,0:T(8,128)(2,1)}, bf16[2,512,768]{2,1,0:T(8,128)(2,1)}, u32[]{:S(2)}, u32[]{:S(2)}) collective-permute-start(bf16[2,512,768]{2,1,0:T(8,128)(2,1)} %collective-permute-done), channel_id=1, source_target_pairs={{0,8},{8,16},{16,24},{24,32},{32,40},{40,48},{48,56},{56,64},{64,7... | collective-permute-start | bytes 4718600 | tf_op jit(solution)/shard_map/ppermute | solution.py:15
  197.9 49.2 %copy-start.2 = (bf16[512,768]{1,0:T(8,128)(2,1)S(1)}, bf16[512,768]{1,0:T(8,128)(2,1)}, u32[]{:S(2)}) copy-start(bf16[512,768]{1,0:T(8,128)(2,1)} %param.17) | copy-start | bytes 2359300
  197.9 49.2 %copy-start.3 = (bf16[512,768]{1,0:T(8,128)(2,1)S(1)}, bf16[512,768]{1,0:T(8,128)(2,1)}, u32[]{:S(2)}) copy-start(bf16[512,768]{1,0:T(8,128)(2,1)} %param.16) | copy-start | bytes 2359300
  197.9 49.2 %collective-permute-start.2 = (bf16[2,512,768]{2,1,0:T(8,128)(2,1)}, bf16[2,512,768]{2,1,0:T(8,128)(2,1)S(1)}, u32[]{:S(2)}, u32[]{:S(2)}) collective-permute-start(bf16[2,512,768]{2,1,0:T(8,128)(2,1)} %collective-permute-done.1), channel_id=1, source_target_pairs={{0,8},{8,16},{16,24},{24,32},{32,40},{40,48},{48,56},{56,64},{64,7... | collective-permute-start | bytes 4718600 | tf_op jit(solution)/shard_map/ppermute | solution.py:15
  259.7 14.4 %copy-start.1 = (bf16[1,2048,768]{1,2,0:T(8,128)(2,1)S(1)}, bf16[1,2048,768]{1,2,0:T(8,128)(2,1)}, u32[]{:S(2)}) copy-start(bf16[1,2048,768]{1,2,0:T(8,128)(2,1)} %copy.63) | copy-start | bytes 9437188
Sparse Core Ops, SparseCore 0:
  70.5 114.5 all-gather.3
  198.0 39.6 reduce-scatter.1
where the time goes:
time: 306 us; the launch traced here: 303 us
  waiting for transfers between devices  88.1 us (29%)
  local copies, waits for them, and re-layouts  66.2 us (22%)
  blocking collectives  52.6 us (17%)
  matrix products  49.9 us (16%)
  other arithmetic  21 us (7%)
  between operations  14.2 us (5%)
  starting transfers between devices  10.4 us (3%)
    all_gather x1, blocking collectives, per_device(): totals = lax.all_gather(device_total[None, :], 'ctx', axis=0, tiled=True)  52.6 us
    all_gather x1, waiting for transfers between devices, per_device(): lax.all_gather(state_dev[None].astype(jnp.bfloat16), 'ctx', axis=0, tiled...  45.3 us
    ppermute x3, waiting for transfers between devices, passed_along(): lax.ppermute(value, axis, [(source, source + steps) for source in range(i...  42.9 us
    dynamic_update_slice x4, local copies, waits for them, and re-layouts, per_device(): state_dev, outputs = lax.scan(block_step, empty_state, inputs)  35 us
    dot_general x1, matrix products, attend_block(): jnp.einsum('hij,jhd->ihd', probability, value_part, preferred_element_typ...  19.3 us
    sub x1, matrix products, attend_block(): exponent = jnp.exp(scores - row_peak)  14.4 us
    ppermute x3, starting transfers between devices, passed_along(): lax.ppermute(value, axis, [(source, source + steps) for source in range(i...  10.3 us
    unnamed x14, local copies, waits for them, and re-layouts  7.93 us
  transfers between devices with their start and end apart: 5, of which 2 were waited for; matrix products, arithmetic and copies ran while one was open for 24% of the time, Pallas kernels for 0%

commit v1 on v0

--- a/solution.py
+++ b/solution.py
@@ -60,7 +60,10 @@
     decay_dev = jnp.cumsum(log_decay, axis=0)
     device_total = decay_dev[-1]
     position = lax.axis_index("ctx")
-    totals = lax.all_gather(device_total[None, :], "ctx", axis=0, tiled=True)
+    totals = jnp.concatenate(
+        lax.all_to_all(jnp.stack([device_total[None, :]] * lax.axis_size("ctx")), "ctx", 0, 0),
+        axis=0,
+    )
     device_ids = jnp.arange(totals.shape[0], dtype=jnp.int32)[:, None]
     earlier_rows = device_ids < position
     running = jnp.cumsum(totals, axis=0)

time: 306 us -> 294 us (0.961)
  blocking collectives: 52.6 us -> 0 us
  waiting for transfers between devices: 88.1 us -> 118 us
  starting transfers between devices: 10.4 us -> 20.3 us
    all_gather x1 -> x0, blocking collectives: 52.6 us -> none  [per_device(): totals = lax.all_gather(device_total[None, :], 'ctx', axis=0, tiled=True)]
    all_to_all x0 -> x1, waiting for transfers between devices: none -> 15.2 us  [per_device(): lax.all_to_all(jnp.stack([device_total[None, :]] * lax.axis_size('ctx')),...]
    all_gather x1, waiting for transfers between devices: 45.3 us -> 59.9 us  [per_device(): lax.all_gather(state_dev[None].astype(jnp.bfloat16), 'ctx', axis=0, tiled...]
    all_to_all x0 -> x1, starting transfers between devices: none -> 8.96 us  [per_device(): lax.all_to_all(jnp.stack([device_total[None, :]] * lax.axis_size('ctx')),...]
  transfers between devices with their start and end apart: 5 -> 6, of which waited for: 2 -> 3; matrix products, arithmetic and copies ran while one was open for 24% -> 26% of each run, Pallas kernels for 0% -> 0%
where the time goes in v1:
time: 294 us; the launch traced here: 290 us
  waiting for transfers between devices  118 us (40%)
  local copies, waits for them, and re-layouts  66.8 us (23%)
  matrix products  49.9 us (17%)
  other arithmetic  21 us (7%)
  starting transfers between devices  20.3 us (7%)
  between operations  14.3 us (5%)
    all_gather x1, waiting for transfers between devices, per_device(): lax.all_gather(state_dev[None].astype(jnp.bfloat16), 'ctx', axis=0, tiled...  59.9 us
    ppermute x3, waiting for transfers between devices, passed_along(): lax.ppermute(value, axis, [(source, source + steps) for source in range(i...  42.8 us
    dynamic_update_slice x4, local copies, waits for them, and re-layouts, per_device(): state_dev, outputs = lax.scan(block_step, empty_state, inputs)  35 us
    dot_general x1, matrix products, attend_block(): jnp.einsum('hij,jhd->ihd', probability, value_part, preferred_element_typ...  19.3 us
    all_to_all x1, waiting for transfers between devices, per_device(): lax.all_to_all(jnp.stack([device_total[None, :]] * lax.axis_size('ctx')),...  15.2 us
    sub x1, matrix products, attend_block(): exponent = jnp.exp(scores - row_peak)  14.4 us
    ppermute x3, starting transfers between devices, passed_along(): lax.ppermute(value, axis, [(source, source + steps) for source in range(i...  11.3 us
    all_to_all x1, starting transfers between devices, per_device(): lax.all_to_all(jnp.stack([device_total[None, :]] * lax.axis_size('ctx')),...  8.96 us
  transfers between devices with their start and end apart: 6, of which 3 were waited for; matrix products, arithmetic and copies ran while one was open for 26% of the time, Pallas kernels for 0%

profile of v1, /device:TPU:1, one launch (start us, length us, event | category | flops | bytes accessed | tf_op | source)
XLA Modules:
  0.0 290.3 jit_solution(1802006850435013422)
XLA Ops:
  7.2 2.2 reshape.203
  10.2 2.2 reshape.204
  13.1 3.0 %reshape.205 = bf16[2,256,8,96]{3,2,1,0:T(8,128)(2,1)} reshape(bf16[512,768]{1,0:T(8,128)(2,1)} %param.10) | data formatting | bytes 1572864 | tf_op jit(solution)/shard_map/reshape | solution.py:52
  16.1 1.6 copy.57
  17.8 51.9 %while.4 = (s32[]{:T(128)}, f32[8,96,96]{2,1,0:T(8,128)S(1)}, f32[2,256,8,96]{1,0,3,2:T(2,128)}, f32[2,256,8]{1,2,0:T(8,128)}, bf16[2,256,8,96]{1,3,2,0:T(8,128)...) while((s32[]{:T(128)}, f32[8,96,96]{2,1,0:T(8,128)S(1)}, ...), condition=%wide.region_3.4_spmd.clone, body=%wide.region_0.3_spmd.clone.sunk | while | flops 658018304 | bytes 9203808 | solution.py:58
  20.5 1.7 fusion.98
  23.6 1.7 fusion.99
  26.1 16.7 %dynamic_update_slice.9 = f32[2,256,8,96]{1,0,3,2:T(2,128)} dynamic-update-slice(f32[2,256,8,96]{1,0,3,2:T(2,128)} %get-tuple-element.191, f32[1,256,8,96]{1,0,3,2:T(1,128)S(1)} %copy.91, s32[]{:T(128)} %get-tuple-element.189, s32[]{:T(128)} %constant.60.clone.1..sunk, s32[]{:T(128)} %constant.60.clone.1..sunk, s32[]{:T(128)} %constant.60.clone.1..sunk) | dynamic-update-slice | bytes 1572868 | tf_op jit(solution)/shard_map/while/body/jit(dynamic_update_index_in_dim)/dynamic_update_slice | solution.py:58
  46.4 1.7 fusion.98
  49.5 1.7 fusion.99
  52.0 16.7 %dynamic_update_slice.9 = f32[2,256,8,96]{1,0,3,2:T(2,128)} dynamic-update-slice(f32[2,256,8,96]{1,0,3,2:T(2,128)} %get-tuple-element.191, f32[1,256,8,96]{1,0,3,2:T(1,128)S(1)} %copy.91, s32[]{:T(128)} %get-tuple-element.189, s32[]{:T(128)} %constant.60.clone.1..sunk, s32[]{:T(128)} %constant.60.clone.1..sunk, s32[]{:T(128)} %constant.60.clone.1..sunk) | dynamic-update-slice | bytes 1572868 | tf_op jit(solution)/shard_map/while/body/jit(dynamic_update_index_in_dim)/dynamic_update_slice | solution.py:58
  70.4 2.7 pad_maximum_fusion
  73.1 6.2 %collective-permute-start = (bf16[2,512,768]{2,1,0:T(8,128)(2,1)}, bf16[2,512,768]{2,1,0:T(8,128)(2,1)}, u32[]{:S(2)}, u32[]{:S(2)}) collective-permute-start(bf16[2,512,768]{2,1,0:T(8,128)(2,1)} %pad_maximum_fusion), channel_id=1, source_target_pairs={{0,8},{8,16},{16,24},{24,32},{32,40},{40,48},{48,56},{56,64},{64,7... | collective-permute-start | bytes 4718600 | tf_op jit(solution)/shard_map/ppermute | solution.py:15
  79.3 2.2 reduce-window.16
  82.6 9.0 %all-to-all-start = ((f32[32,1,8]{2,1,0:T(1,128)}), f32[32,1,8]{2,1,0:T(1,128)S(1)}, u32[]{:S(2)}, u32[]{:S(2)}) async-start(f32[32,1,8]{2,1,0:T(1,128)} %stack.12), calls=%async_computation | async-start | bytes 32768 | tf_op jit(solution)/shard_map/all_to_all | solution.py:64
  91.9 2.5 reshape.190
  94.5 15.2 %all-to-all-done = f32[32,1,8]{2,1,0:T(1,128)S(1)} async-done(((f32[32,1,8]{2,1,0:T(1,128)}), f32[32,1,8]{2,1,0:T(1,128)S(1)}, u32[]{:S(2)}, u32[]{:S(2)}) %all-to-all-start) | async-done | bytes 1056 | tf_op jit(solution)/shard_map/all_to_all | solution.py:64
  109.9 3.0 %collective-permute-start.1 = (bf16[2,512,768]{2,1,0:T(8,128)(2,1)}, bf16[2,512,768]{2,1,0:T(8,128)(2,1)}, u32[]{:S(2)}, u32[]{:S(2)}) collective-permute-start(bf16[2,512,768]{2,1,0:T(8,128)(2,1)} %collective-permute-done), channel_id=1, source_target_pairs={{0,8},{8,16},{16,24},{24,32},{32,40},{40,48},{48,56},{56,64},{64,7... | collective-permute-start | bytes 4718600 | tf_op jit(solution)/shard_map/ppermute | solution.py:15
  112.9 59.9 %all-gather.3.cloned.1.call-done = bf16[256,96,96]{2,1,0:T(8,128)(2,1)} async-done(((bf16[8,96,96]{2,1,0:T(8,128)(2,1)}), bf16[256,96,96]{2,1,0:T(8,128)(2,1)}) %all-gather.3.cloned.1.call-update) | async-done | bytes 4718608 | tf_op jit(solution)/shard_map/all_gather | solution.py:75
  172.8 4.5 %multiply_reduce_fusion = f32[8,96,96]{2,1,0:T(8,128)S(1)} fusion(bf16[8,32,96,96]{3,2,0,1:T(8,128)(2,1)} %bitcast.130, f32[8,32]{0,1:T(8,128)S(1)} %exponential_bitcast_fusion), kind=kLoop, calls=%fused_computation.53 | loop fusion | flops 7004160 | bytes 5014528 | tf_op jit(solution)/shard_map/nh,nhde->hde/dot_general | solution.py:72
  179.2 6.4 %convolution_convert_fusion = bf16[512,3072]{1,0:T(8,128)(2,1)} fusion(bf16[512,768]{0,1:T(8,128)(2,1)S(1)} %bitcast.142, bf16[768,3072]{1,0:T(8,128)(2,1)} %param.14), kind=kOutput, calls=%fused_computation.57 | convolution fusion | flops 2417491968 | bytes 8650752 | tf_op jit(solution)/shard_map/dot_general | solution.py:95
  185.6 2.1 collective-permute-start.2
  187.7 2.3 copy.62
  190.0 2.0 fusion.46
  192.0 42.8 %collective-permute-done.2 = bf16[2,512,768]{2,1,0:T(8,128)(2,1)S(1)} collective-permute-done((bf16[2,512,768]{2,1,0:T(8,128)(2,1)}, bf16[2,512,768]{2,1,0:T(8,128)(2,1)S(1)}, u32[]{:S(2)}, u32[]{:S(2)}) %collective-permute-start.2) | collective-permute-done | bytes 1572896 | tf_op jit(solution)/shard_map/ppermute | solution.py:15
  234.8 2.8 maximum_maximum_fusion
  237.6 2.1 fusion.66
  239.7 4.7 %copy.61 = bf16[1,2048,768]{1,2,0:T(8,128)(2,1)} copy(bf16[1,2048,768]{2,1,0:T(8,128)(2,1)} %get-tuple-element.128) | data formatting | bytes 6291456 | tf_op jit(solution)/shard_map/while/body/eval_jaxpr/slice | solution.py:116
  244.5 3.0 %copy.60 = bf16[1,2048,768]{1,2,0:T(8,128)(2,1)} copy(bf16[1,2048,768]{2,1,0:T(8,128)(2,1)S(1)} %get-tuple-element.129) | data formatting | bytes 6291456 | tf_op jit(solution)/shard_map/while/body/eval_jaxpr/slice | solution.py:117
  247.4 14.4 %fusion.67 = f32[8,512]{1,0:T(8,128)S(1)} fusion(pred[512,2048]{0,1:T(8,128)(4,1)} %fusion.46, bf16[2048,8,96]{0,2,1:T(8,128)(2,1)} %bitcast.131, bf16[512,8,96]{0,2,1:T(8,128)(2,1)} %bitcast.139), kind=kOutput, calls=%fused_computation.85 | convolution fusion | flops 1644169216 | bytes 4997120 | tf_op jit(solution)/shard_map/while/body/eval_jaxpr/sub | solution.py:129
  261.9 19.3 %fusion.54 = bf16[8,96,512]{2,1,0:T(8,128)(2,1)} fusion(bf16[2048,8,96]{0,2,1:T(8,128)(2,1)S(1)} %bitcast.133, f32[8,512]{1,0:T(8,128)S(1)} %fusion.67, pred[512,2048]{0,1:T(8,128)(4,1)} %fusion.46, bf16[2048,8,96]{0,2,1:T(8,128)(2,1)} %bitcast.132, bf16[512,8,96]{0,2,1:T(8,128)(2,1)} %bitcast.140), kind=kOutput, calls=%fused_computation.67 | convolution fusion | flops 3263567872 | bytes 8929280 | tf_op jit(solution)/shard_map/while/body/eval_jaxpr/hij,jhd->ihd/dot_general | solution.py:131
  281.2 2.3 copy.64
  (66 shorter events, 17.4 us)
Async XLA Ops:
  7.2 165.7 %all-gather.3.cloned.1.call-start = ((), (), s32[]{:S(2)}) async-start(), calls=%async_computation.3 | async-start | bytes 6488064 | tf_op jit(solution)/shard_map/all_gather | solution.py:75
  19.3 0.6 copy-start.4
  45.2 0.6 copy-start.4
  69.7 22.0 %copy-start = (bf16[512,768]{1,0:T(8,128)(2,1)S(1)}, bf16[512,768]{1,0:T(8,128)(2,1)}, u32[]{:S(2)}) copy-start(bf16[512,768]{1,0:T(8,128)(2,1)} %param.10) | copy-start | bytes 2359300
  73.1 36.8 %collective-permute-start = (bf16[2,512,768]{2,1,0:T(8,128)(2,1)}, bf16[2,512,768]{2,1,0:T(8,128)(2,1)}, u32[]{:S(2)}, u32[]{:S(2)}) collective-permute-start(bf16[2,512,768]{2,1,0:T(8,128)(2,1)} %pad_maximum_fusion), channel_id=1, source_target_pairs={{0,8},{8,16},{16,24},{24,32},{32,40},{40,48},{48,56},{56,64},{64,7... | collective-permute-start | bytes 4718600 | tf_op jit(solution)/shard_map/ppermute | solution.py:15
  82.6 27.1 %all-to-all-start = ((f32[32,1,8]{2,1,0:T(1,128)}), f32[32,1,8]{2,1,0:T(1,128)S(1)}, u32[]{:S(2)}, u32[]{:S(2)}) async-start(f32[32,1,8]{2,1,0:T(1,128)} %stack.12), calls=%async_computation | async-start | bytes 32768 | tf_op jit(solution)/shard_map/all_to_all | solution.py:64
  91.6 191.9 %reduce-scatter.2.cloned.1.call-start = ((), (), s32[]{:S(2)}) async-start(), calls=%async_computation.2 | async-start | bytes 3538944 | tf_op jit(solution)/shard_map/reduce_scatter | solution.py:94
  109.9 75.7 %collective-permute-start.1 = (bf16[2,512,768]{2,1,0:T(8,128)(2,1)}, bf16[2,512,768]{2,1,0:T(8,128)(2,1)}, u32[]{:S(2)}, u32[]{:S(2)}) collective-permute-start(bf16[2,512,768]{2,1,0:T(8,128)(2,1)} %collective-permute-done), channel_id=1, source_target_pairs={{0,8},{8,16},{16,24},{24,32},{32,40},{40,48},{48,56},{56,64},{64,7... | collective-permute-start | bytes 4718600 | tf_op jit(solution)/shard_map/ppermute | solution.py:15
  185.6 49.2 %copy-start.2 = (bf16[512,768]{1,0:T(8,128)(2,1)S(1)}, bf16[512,768]{1,0:T(8,128)(2,1)}, u32[]{:S(2)}) copy-start(bf16[512,768]{1,0:T(8,128)(2,1)} %param.17) | copy-start | bytes 2359300
  185.6 49.2 %copy-start.3 = (bf16[512,768]{1,0:T(8,128)(2,1)S(1)}, bf16[512,768]{1,0:T(8,128)(2,1)}, u32[]{:S(2)}) copy-start(bf16[512,768]{1,0:T(8,128)(2,1)} %param.16) | copy-start | bytes 2359300
  185.6 49.2 %collective-permute-start.2 = (bf16[2,512,768]{2,1,0:T(8,128)(2,1)}, bf16[2,512,768]{2,1,0:T(8,128)(2,1)S(1)}, u32[]{:S(2)}, u32[]{:S(2)}) collective-permute-start(bf16[2,512,768]{2,1,0:T(8,128)(2,1)} %collective-permute-done.1), channel_id=1, source_target_pairs={{0,8},{8,16},{16,24},{24,32},{32,40},{40,48},{48,56},{56,64},{64,7... | collective-permute-start | bytes 4718600 | tf_op jit(solution)/shard_map/ppermute | solution.py:15
  247.4 14.4 %copy-start.1 = (bf16[1,2048,768]{1,2,0:T(8,128)(2,1)S(1)}, bf16[1,2048,768]{1,2,0:T(8,128)(2,1)}, u32[]{:S(2)}) copy-start(bf16[1,2048,768]{1,2,0:T(8,128)(2,1)} %copy.60) | copy-start | bytes 9437188
Sparse Core Ops, SparseCore 0:
  70.5 102.2 all-gather.2
  185.7 42.6 reduce-scatter.1
